TPU v7x, 32 devices: a whole 2x2x4 slice. The times are simulated.
32 devices in a mesh: tm: 8 (over y, x, core), space: 4 (over z).
Axes of the slice: x: 2, y: 2, z: 4, core: 2. Of those that a mesh axis runs over, the one named last changes fastest.
Arguments:
- steps: bfloat16 [24, 1024, 1024], P('tm', 'space'), as said below
- lengths: int32 [8], P('tm'), may hold values from 1 to 3, 16 in all
- anchor: bfloat16 [1024, 2048], P(None, 'space'), may hold values from -6 to 6
Outputs:
- panels: float32 [24, 1024, 2048], P('tm', None, 'space')
Inputs may be any that keep to these rules, and one draw needn't show every extreme that they name: `steps`: slots of a section beyond its length hold entries that no output reads.
All inputs are finite; a program needn't handle non-finite values. No bound on the sum of `lengths` on one device may be relied on, other than what follows from the above.
Results may differ from a plain program's by a relative error of at most 0.025.
Values may be sent and summed in bfloat16 or wider, within the bound.
A program may use at most 64 MiB of HBM per device.

v0:
```python
import jax
import jax.numpy as jnp
from jax import lax
from jax.sharding import PartitionSpec as P


def from_behind(block, axis, distance):
    devices = range(lax.axis_size(axis))
    route = [(i - distance, i) for i in devices if i - distance in devices]
    return lax.ppermute(block, axis, route)


def run_section(blocks, section_count, incoming, results, offset):
    capacity = blocks.shape[0]
    for slot in range(capacity - 1, -1, -1):

        def live(state, slot=slot):
            carry_in, stored = state
            value = jnp.dot(blocks[slot], carry_in, preferred_element_type=jnp.float32)
            stored = lax.dynamic_update_slice(stored, value[None], (slot, 0, offset))
            return (value.astype(jnp.bfloat16), stored)

        incoming, results = lax.cond(
            slot < section_count, live, lambda state: state, (incoming, results)
        )
    return (incoming, results)


def shards(steps, lengths, anchor):
    capacity, width = (steps.shape[0], anchor.shape[1])
    rows = anchor.shape[0]
    segments = lax.axis_size("tm")
    me = lax.axis_index("tm")
    section_count = lengths[0]
    blocks = lax.all_gather(steps, "space", axis=1, tiled=True)
    results = jnp.zeros((capacity, rows, width), jnp.float32)

    def segment(k, state):
        incoming, stored = state
        active = me == segments - 1 - k
        incoming, stored = lax.cond(
            active,
            lambda s: run_section(blocks, section_count, s[0], s[1], 0),
            lambda s: s,
            (incoming, stored),
        )
        incoming = from_behind(incoming, "tm", -1)
        return (incoming, stored)

    final, results = lax.fori_loop(0, segments, segment, (anchor, results))
    return results


def solution(mesh):
    return jax.shard_map(
        shards,
        mesh=mesh,
        in_specs=(P("tm", "space", None), P("tm"), P(None, "space")),
        out_specs=P("tm", None, "space"),
        check_vma=False,
    )
```

profile of v0, /device:TPU:3, one launch (start us, length us, event | category | flops | bytes accessed | tf_op | source)
XLA Modules:
  0.0 303.0 jit_solution(14158469819239776622)
XLA Ops:
  6.5 0.0 copy-start
  6.5 0.0 all-gather.2.cloned.1.call-start
  6.5 0.7 all-gather.2.cloned.1.call-update
  7.3 118.4 %all-gather.2.cloned.1.call-done = bf16[3,1024,1024]{2,1,0:T(8,128)(2,1)} async-done(((bf16[3,256,1024]{2,1,0:T(8,128)(2,1)}), bf16[3,1024,1024]{2,1,0:T(8,128)(2,1)}) %all-gather.2.cloned.1.call-update) | async-done | bytes 6291472 | tf_op jit(solution)/shard_map/all_gather | solution.py:35
  125.7 3.5 %broadcast_in_dim.12 = f32[3,1024,512]{2,1,0:T(8,128)} broadcast(f32[]{:T(128)} %constant.39.clone.1), dimensions={} | broadcast | bytes 6291460 | tf_op jit(solution)/shard_map/broadcast_in_dim | solution.py:36
  129.2 0.0 copy-done
  129.2 167.0 %while.15 = (s32[]{:T(128)}, bf16[1024,512]{1,0:T(8,128)(2,1)S(1)}, f32[3,1024,512]{2,1,0:T(8,128)}, s32[]{:T(128)}, s32[]{:T(128)}, /*index=5*/bf16[3,1024,1024]{2,1,0:T(8,128)(2,1)}, s32[]{:T(128)}, s32[]{:T(128)}) while((s32[]{:T(128)}, bf16[1024,512]{1,0:T(8,128)(2,1)S(1)}, f32[3,1024,512]{2,1,0:T(8,128)}, s32[]{:T(128)}, s32[]{:T(128)}, ...), condition=%wide.region_9.0_spmd, body=%wide.region_0.0_spmd.sunk | while | flops 3222798336 | bytes 44040592 | solution.py:50
  129.2 2.4 collective-permute-start
  131.6 14.6 %collective-permute-done = bf16[1024,512]{1,0:T(8,128)(2,1)S(1)} collective-permute-done((bf16[1024,512]{1,0:T(8,128)(2,1)S(1)}, bf16[1024,512]{1,0:T(8,128)(2,1)S(1)}, u32[]{:S(2)}, u32[]{:S(2)}) %collective-permute-start) | collective-permute-done | bytes 1048608 | tf_op jit(solution)/shard_map/while/body/eval_jaxpr/ppermute | solution.py:10
  146.2 0.1 copy.30
  146.3 1.9 collective-permute-start
  148.2 15.1 %collective-permute-done = bf16[1024,512]{1,0:T(8,128)(2,1)S(1)} collective-permute-done((bf16[1024,512]{1,0:T(8,128)(2,1)S(1)}, bf16[1024,512]{1,0:T(8,128)(2,1)S(1)}, u32[]{:S(2)}, u32[]{:S(2)}) %collective-permute-start) | collective-permute-done | bytes 1048608 | tf_op jit(solution)/shard_map/while/body/eval_jaxpr/ppermute | solution.py:10
  163.3 0.1 copy.30
  163.4 1.9 collective-permute-start
  165.4 15.1 %collective-permute-done = bf16[1024,512]{1,0:T(8,128)(2,1)S(1)} collective-permute-done((bf16[1024,512]{1,0:T(8,128)(2,1)S(1)}, bf16[1024,512]{1,0:T(8,128)(2,1)S(1)}, u32[]{:S(2)}, u32[]{:S(2)}) %collective-permute-start) | collective-permute-done | bytes 1048608 | tf_op jit(solution)/shard_map/while/body/eval_jaxpr/ppermute | solution.py:10
  180.4 0.1 copy.30
  180.6 1.9 collective-permute-start
  182.5 29.8 %collective-permute-done = bf16[1024,512]{1,0:T(8,128)(2,1)S(1)} collective-permute-done((bf16[1024,512]{1,0:T(8,128)(2,1)S(1)}, bf16[1024,512]{1,0:T(8,128)(2,1)S(1)}, u32[]{:S(2)}, u32[]{:S(2)}) %collective-permute-start) | collective-permute-done | bytes 1048608 | tf_op jit(solution)/shard_map/while/body/eval_jaxpr/ppermute | solution.py:10
  212.3 0.1 copy.30
  212.4 15.3 %conditional.5 = ((bf16[1024,512]{1,0:T(8,128)(2,1)S(1)}, f32[3,1024,512]{2,1,0:T(8,128)})) conditional(s32[]{:T(128)} %convert_element_type.29, (bf16[1024,512]{1,0:T(8,128)(2,1)S(1)}, f32[3,1024,512]{2,1,0:T(8,128)}) %tuple.58, (s32[]{:T(128)}, bf16[1024,512]{1,0:T(8,128)(2,1)S(1)}, f32[3,1024,512]{2,1,0:T(8,128)}, ...), branch_computations={%region_1.0_spmd, %region_2.0_spmd} | conditional | flops 3222798336 | bytes 37748936 | solution.py:41
  213.1 4.4 %conditional = ((bf16[1024,512]{1,0:T(8,128)(2,1)S(1)}, f32[3,1024,512]{2,1,0:T(8,128)})) conditional(s32[]{:T(128)} %convert_element_type.23, (bf16[1024,512]{1,0:T(8,128)(2,1)S(1)}, f32[3,1024,512]{2,1,0:T(8,128)}) %tuple.36, (bf16[3,1024,1024]{2,1,0:T(8,128)(2,1)}, bf16[1024,512]{1,0:T(8,128)(2,1)S(1)}, f32[3,1024,512]{2,1,0:T(8,128)}) %tuple.37), branch_computations={%region_3.0_spmd, %region_4.0_spmd} | conditional | flops 1074266112 | bytes 12582936 | solution.py:23
  213.1 0.1 copy.32
  213.2 2.8 fusion.9
  216.0 1.5 bitcast_dynamic-update-slice_fusion
  218.2 4.4 %conditional.1 = ((bf16[1024,512]{1,0:T(8,128)(2,1)S(1)}, f32[3,1024,512]{2,1,0:T(8,128)})) conditional(s32[]{:T(128)} %convert_element_type.22, (bf16[1024,512]{1,0:T(8,128)(2,1)S(1)}, f32[3,1024,512]{2,1,0:T(8,128)}) %get-tuple-element.277, (bf16[3,1024,1024]{2,1,0:T(8,128)(2,1)}, bf16[1024,512]{1,0:T(8,128)(2,1)S(1)}, ...), branch_computations={%region_5.0_spmd, %region_6.0_spmd} | conditional | flops 1074266112 | bytes 12582936 | solution.py:23
  218.2 0.1 copy.33
  218.3 2.8 fusion.10
  221.1 1.5 bitcast_dynamic-update-slice_fusion.1
  223.3 4.4 %conditional.2 = ((bf16[1024,512]{1,0:T(8,128)(2,1)S(1)}, f32[3,1024,512]{2,1,0:T(8,128)})) conditional(s32[]{:T(128)} %convert_element_type.21, (bf16[1024,512]{1,0:T(8,128)(2,1)S(1)}, f32[3,1024,512]{2,1,0:T(8,128)}) %get-tuple-element.278, (bf16[3,1024,1024]{2,1,0:T(8,128)(2,1)}, bf16[1024,512]{1,0:T(8,128)(2,1)S(1)}, ...), branch_computations={%region_7.0_spmd, %region_8.0_spmd} | conditional | flops 1074266112 | bytes 12582936 | solution.py:23
  223.3 0.1 copy.34
  223.3 2.8 fusion.11
  226.2 1.5 bitcast_dynamic-update-slice_fusion.2
  227.7 1.9 collective-permute-start
  229.6 15.1 %collective-permute-done = bf16[1024,512]{1,0:T(8,128)(2,1)S(1)} collective-permute-done((bf16[1024,512]{1,0:T(8,128)(2,1)S(1)}, bf16[1024,512]{1,0:T(8,128)(2,1)S(1)}, u32[]{:S(2)}, u32[]{:S(2)}) %collective-permute-start) | collective-permute-done | bytes 1048608 | tf_op jit(solution)/shard_map/while/body/eval_jaxpr/ppermute | solution.py:10
  244.7 0.1 copy.30
  244.8 1.9 collective-permute-start
  246.7 15.1 %collective-permute-done = bf16[1024,512]{1,0:T(8,128)(2,1)S(1)} collective-permute-done((bf16[1024,512]{1,0:T(8,128)(2,1)S(1)}, bf16[1024,512]{1,0:T(8,128)(2,1)S(1)}, u32[]{:S(2)}, u32[]{:S(2)}) %collective-permute-start) | collective-permute-done | bytes 1048608 | tf_op jit(solution)/shard_map/while/body/eval_jaxpr/ppermute | solution.py:10
  261.8 0.1 copy.30
  262.0 1.9 collective-permute-start
  263.9 15.1 %collective-permute-done = bf16[1024,512]{1,0:T(8,128)(2,1)S(1)} collective-permute-done((bf16[1024,512]{1,0:T(8,128)(2,1)S(1)}, bf16[1024,512]{1,0:T(8,128)(2,1)S(1)}, u32[]{:S(2)}, u32[]{:S(2)}) %collective-permute-start) | collective-permute-done | bytes 1048608 | tf_op jit(solution)/shard_map/while/body/eval_jaxpr/ppermute | solution.py:10
  279.0 0.1 copy.30
  279.1 1.9 collective-permute-start
  281.0 15.1 %collective-permute-done = bf16[1024,512]{1,0:T(8,128)(2,1)S(1)} collective-permute-done((bf16[1024,512]{1,0:T(8,128)(2,1)S(1)}, bf16[1024,512]{1,0:T(8,128)(2,1)S(1)}, u32[]{:S(2)}, u32[]{:S(2)}) %collective-permute-start) | collective-permute-done | bytes 1048608 | tf_op jit(solution)/shard_map/while/body/eval_jaxpr/ppermute | solution.py:10
  296.1 0.1 copy.30
  (7 shorter events, 0.1 us)
Async XLA Ops:
  6.5 122.6 %copy-start = (bf16[1024,512]{1,0:T(8,128)(2,1)S(1)}, bf16[1024,512]{1,0:T(8,128)(2,1)}, u32[]{:S(2)}) copy-start(bf16[1024,512]{1,0:T(8,128)(2,1)} %param.15) | copy-start | bytes 3145732
  6.5 119.1 %all-gather.2.cloned.1.call-start = ((), (), s32[]{:S(2)}) async-start(), calls=%async_computation | async-start | bytes 7864320 | tf_op jit(solution)/shard_map/all_gather | solution.py:35
  129.2 17.0 %collective-permute-start = (bf16[1024,512]{1,0:T(8,128)(2,1)S(1)}, bf16[1024,512]{1,0:T(8,128)(2,1)S(1)}, u32[]{:S(2)}, u32[]{:S(2)}) collective-permute-start(bf16[1024,512]{1,0:T(8,128)(2,1)S(1)} %get-tuple-element.235), channel_id=1, source_target_pairs={{4,0},{8,4},{12,8},{16,12},{20,16},{24,20},{28,24},{5,1},{9,5},{13... | collective-permute-start | bytes 3145736 | tf_op jit(solution)/shard_map/while/body/eval_jaxpr/ppermute | solution.py:10
  146.3 17.0 %collective-permute-start = (bf16[1024,512]{1,0:T(8,128)(2,1)S(1)}, bf16[1024,512]{1,0:T(8,128)(2,1)S(1)}, u32[]{:S(2)}, u32[]{:S(2)}) collective-permute-start(bf16[1024,512]{1,0:T(8,128)(2,1)S(1)} %get-tuple-element.235), channel_id=1, source_target_pairs={{4,0},{8,4},{12,8},{16,12},{20,16},{24,20},{28,24},{5,1},{9,5},{13... | collective-permute-start | bytes 3145736 | tf_op jit(solution)/shard_map/while/body/eval_jaxpr/ppermute | solution.py:10
  163.4 17.0 %collective-permute-start = (bf16[1024,512]{1,0:T(8,128)(2,1)S(1)}, bf16[1024,512]{1,0:T(8,128)(2,1)S(1)}, u32[]{:S(2)}, u32[]{:S(2)}) collective-permute-start(bf16[1024,512]{1,0:T(8,128)(2,1)S(1)} %get-tuple-element.235), channel_id=1, source_target_pairs={{4,0},{8,4},{12,8},{16,12},{20,16},{24,20},{28,24},{5,1},{9,5},{13... | collective-permute-start | bytes 3145736 | tf_op jit(solution)/shard_map/while/body/eval_jaxpr/ppermute | solution.py:10
  180.6 31.8 %collective-permute-start = (bf16[1024,512]{1,0:T(8,128)(2,1)S(1)}, bf16[1024,512]{1,0:T(8,128)(2,1)S(1)}, u32[]{:S(2)}, u32[]{:S(2)}) collective-permute-start(bf16[1024,512]{1,0:T(8,128)(2,1)S(1)} %get-tuple-element.235), channel_id=1, source_target_pairs={{4,0},{8,4},{12,8},{16,12},{20,16},{24,20},{28,24},{5,1},{9,5},{13... | collective-permute-start | bytes 3145736 | tf_op jit(solution)/shard_map/while/body/eval_jaxpr/ppermute | solution.py:10
  227.7 17.0 %collective-permute-start = (bf16[1024,512]{1,0:T(8,128)(2,1)S(1)}, bf16[1024,512]{1,0:T(8,128)(2,1)S(1)}, u32[]{:S(2)}, u32[]{:S(2)}) collective-permute-start(bf16[1024,512]{1,0:T(8,128)(2,1)S(1)} %get-tuple-element.235), channel_id=1, source_target_pairs={{4,0},{8,4},{12,8},{16,12},{20,16},{24,20},{28,24},{5,1},{9,5},{13... | collective-permute-start | bytes 3145736 | tf_op jit(solution)/shard_map/while/body/eval_jaxpr/ppermute | solution.py:10
  244.8 17.0 %collective-permute-start = (bf16[1024,512]{1,0:T(8,128)(2,1)S(1)}, bf16[1024,512]{1,0:T(8,128)(2,1)S(1)}, u32[]{:S(2)}, u32[]{:S(2)}) collective-permute-start(bf16[1024,512]{1,0:T(8,128)(2,1)S(1)} %get-tuple-element.235), channel_id=1, source_target_pairs={{4,0},{8,4},{12,8},{16,12},{20,16},{24,20},{28,24},{5,1},{9,5},{13... | collective-permute-start | bytes 3145736 | tf_op jit(solution)/shard_map/while/body/eval_jaxpr/ppermute | solution.py:10
  262.0 17.0 %collective-permute-start = (bf16[1024,512]{1,0:T(8,128)(2,1)S(1)}, bf16[1024,512]{1,0:T(8,128)(2,1)S(1)}, u32[]{:S(2)}, u32[]{:S(2)}) collective-permute-start(bf16[1024,512]{1,0:T(8,128)(2,1)S(1)} %get-tuple-element.235), channel_id=1, source_target_pairs={{4,0},{8,4},{12,8},{16,12},{20,16},{24,20},{28,24},{5,1},{9,5},{13... | collective-permute-start | bytes 3145736 | tf_op jit(solution)/shard_map/while/body/eval_jaxpr/ppermute | solution.py:10
  279.1 17.0 %collective-permute-start = (bf16[1024,512]{1,0:T(8,128)(2,1)S(1)}, bf16[1024,512]{1,0:T(8,128)(2,1)S(1)}, u32[]{:S(2)}, u32[]{:S(2)}) collective-permute-start(bf16[1024,512]{1,0:T(8,128)(2,1)S(1)} %get-tuple-element.235), channel_id=1, source_target_pairs={{4,0},{8,4},{12,8},{16,12},{20,16},{24,20},{28,24},{5,1},{9,5},{13... | collective-permute-start | bytes 3145736 | tf_op jit(solution)/shard_map/while/body/eval_jaxpr/ppermute | solution.py:10
Sparse Core Ops, SparseCore 0:
  8.9 116.7 all-gather.1
where the time goes:
time: 303 us
  waiting for transfers between devices  254 us (84%)
  starting transfers between devices  15.8 us (5%)
  between operations  13.4 us (4%)
  local copies, waits for them, and re-layouts  8.74 us (3%)
  matrix products  8.52 us (3%)
    ppermute x8, waiting for transfers between devices, from_behind(): return lax.ppermute(block, axis, route)  135 us
    all_gather x1, waiting for transfers between devices, shards(): blocks = lax.all_gather(steps, 'space', axis=1, tiled=True)  118 us
    ppermute x8, starting transfers between devices, from_behind(): return lax.ppermute(block, axis, route)  15.8 us
    dot_general x3, matrix products, live(): value = jnp.dot(blocks[slot], carry_in, preferred_element_type=jnp.float32)  8.52 us
  transfers between devices with their start and end apart: 9, of which 9 were waited for; matrix products, arithmetic and copies ran while one was open for 0% of the time, Pallas kernels for 0%

commit v1 on v0

--- a/solution.py
+++ b/solution.py
@@ -32,7 +32,14 @@
     segments = lax.axis_size("tm")
     me = lax.axis_index("tm")
     section_count = lengths[0]
-    blocks = lax.all_gather(steps, "space", axis=1, tiled=True)
+    size = lax.axis_size("space")
+    route_2 = [(i_2, (i_2 + 1) % size) for i_2 in range(size)]
+    shards_2 = [steps]
+    for far in range(1, size):
+        shards_2 = [lax.ppermute(shards_2[0], "space", route_2), *shards_2]
+    result = jnp.concatenate(shards_2, axis=1)
+    places = (lax.axis_index("space") + 1) * shards_2[-1].shape[1]
+    blocks = jnp.roll(result, places, axis=1)
     results = jnp.zeros((capacity, rows, width), jnp.float32)
 
     def segment(k, state):

time: 303 us -> 293 us (0.967)
  between operations: 13.4 us -> 0.06 us
  waiting for transfers between devices: 254 us -> 243 us
  local copies, waits for them, and re-layouts: 8.74 us -> 18.7 us
  starting transfers between devices: 15.8 us -> 19.7 us
    all_gather x1 -> x0, waiting for transfers between devices: 118 us -> none  [shards(): blocks = lax.all_gather(steps, 'space', axis=1, tiled=True)]
    ppermute x0 -> x3, waiting for transfers between devices: none -> 109 us  [shards(): shards_2 = [lax.ppermute(shards_2[0], 'space', route_2), *shards_2]]
    unnamed x2 -> x11, local copies, waits for them, and re-layouts: 0.01 us -> 6.48 us
    dynamic_slice x0 -> x1, local copies, waits for them, and re-layouts: none -> 3.38 us  [shards(): blocks = jnp.roll(result, places, axis=1)]
  transfers between devices with their start and end apart: 9 -> 11, of which waited for: 9 -> 11; matrix products, arithmetic and copies ran while one was open for 0% -> 0% of each run, Pallas kernels for 0% -> 0%
where the time goes in v1:
time: 293 us
  waiting for transfers between devices  243 us (83%)
  starting transfers between devices  19.7 us (7%)
  local copies, waits for them, and re-layouts  18.7 us (6%)
  matrix products  8.52 us (3%)
    ppermute x8, waiting for transfers between devices, from_behind(): return lax.ppermute(block, axis, route)  135 us
    ppermute x3, waiting for transfers between devices, shards(): shards_2 = [lax.ppermute(shards_2[0], 'space', route_2), *shards_2]  109 us
    ppermute x8, starting transfers between devices, from_behind(): return lax.ppermute(block, axis, route)  18.4 us
    dot_general x3, matrix products, live(): value = jnp.dot(blocks[slot], carry_in, preferred_element_type=jnp.float32)  8.52 us
    unnamed x11, local copies, waits for them, and re-layouts  6.48 us
  transfers between devices with their start and end apart: 11, of which 11 were waited for; matrix products, arithmetic and copies ran while one was open for 0% of the time, Pallas kernels for 0%

profile of v1, /device:TPU:3, one launch (start us, length us, event | category | flops | bytes accessed | tf_op | source)
XLA Modules:
  0.0 292.9 jit_solution(15430566792756954722)
XLA Ops:
  0.0 1.3 collective-permute-start.1
  1.3 36.3 %collective-permute-done.1 = bf16[3,256,1024]{2,1,0:T(8,128)(2,1)S(1)} collective-permute-done((bf16[3,256,1024]{2,1,0:T(8,128)(2,1)}, bf16[3,256,1024]{2,1,0:T(8,128)(2,1)S(1)}, u32[]{:S(2)}, u32[]{:S(2)}) %collective-permute-start.1) | collective-permute-done | bytes 1572896 | tf_op jit(solution)/shard_map/ppermute | solution.py:39
  37.6 36.5 %collective-permute-done.2 = bf16[3,256,1024]{2,1,0:T(8,128)(2,1)} collective-permute-done((bf16[3,256,1024]{2,1,0:T(8,128)(2,1)S(1)}, bf16[3,256,1024]{2,1,0:T(8,128)(2,1)}, u32[]{:S(2)}, u32[]{:S(2)}) %collective-permute-start.2) | collective-permute-done | bytes 1572896 | tf_op jit(solution)/shard_map/ppermute | solution.py:39
  74.0 35.8 %collective-permute-done.3 = bf16[3,256,1024]{2,1,0:T(8,128)(2,1)} collective-permute-done((bf16[3,256,1024]{2,1,0:T(8,128)(2,1)}, bf16[3,256,1024]{2,1,0:T(8,128)(2,1)}, u32[]{:S(2)}, u32[]{:S(2)}) %collective-permute-start.3) | collective-permute-done | bytes 1572896 | tf_op jit(solution)/shard_map/ppermute | solution.py:39
  109.8 1.5 constant_dynamic-update-slice_fusion.7
  111.4 1.5 constant_dynamic-update-slice_fusion.6
  112.9 0.1 constant_dynamic-update-slice_fusion.5
  113.0 0.1 constant_dynamic-update-slice_fusion.4
  113.2 1.5 constant_dynamic-update-slice_fusion.3
  114.7 1.5 constant_dynamic-update-slice_fusion.2
  116.2 0.1 constant_dynamic-update-slice_fusion.1
  116.3 0.1 constant_dynamic-update-slice_fusion
  116.5 3.4 %constant_dynamic-slice_fusion = bf16[3,1024,1024]{2,1,0:T(8,128)(2,1)} fusion(bf16[3,2048,1024]{2,1,0:T(8,128)(2,1)S(1)} %constant_dynamic-update-slice_fusion, s32[]{:T(128)S(6)} %select_n.14), kind=kLoop, calls=%fused_computation.20 | loop fusion | bytes 12582916 | tf_op jit(solution)/shard_map/jit(_roll_dynamic)/dynamic_slice | solution.py:42
  119.9 3.5 %broadcast_in_dim.12 = f32[3,1024,512]{2,1,0:T(8,128)} broadcast(f32[]{:T(128)} %constant.61.clone.1), dimensions={} | broadcast | bytes 6291460 | tf_op jit(solution)/shard_map/broadcast_in_dim | solution.py:43
  123.4 169.5 %while.15 = (s32[]{:T(128)}, bf16[1024,512]{1,0:T(8,128)(2,1)S(1)}, f32[3,1024,512]{2,1,0:T(8,128)}, s32[]{:T(128)}, s32[]{:T(128)}, /*index=5*/bf16[3,1024,1024]{2,1,0:T(8,128)(2,1)}, s32[]{:T(128)}, s32[]{:T(128)}) while((s32[]{:T(128)}, bf16[1024,512]{1,0:T(8,128)(2,1)S(1)}, f32[3,1024,512]{2,1,0:T(8,128)}, s32[]{:T(128)}, s32[]{:T(128)}, ...), condition=%wide.region_9.10_spmd, body=%wide.region_0.9_spmd.sunk | while | flops 3222798336 | bytes 44040592 | solution.py:57
  123.4 5.0 %collective-permute-start = (bf16[1024,512]{1,0:T(8,128)(2,1)S(1)}, bf16[1024,512]{1,0:T(8,128)(2,1)S(1)}, u32[]{:S(2)}, u32[]{:S(2)}) collective-permute-start(bf16[1024,512]{1,0:T(8,128)(2,1)S(1)} %get-tuple-element.235), channel_id=1, source_target_pairs={{4,0},{8,4},{12,8},{16,12},{20,16},{24,20},{28,24},{5,1},{9,5},{13... | collective-permute-start | bytes 3145736 | tf_op jit(solution)/shard_map/while/body/eval_jaxpr/ppermute | solution.py:10
  128.4 13.6 %collective-permute-done = bf16[1024,512]{1,0:T(8,128)(2,1)S(1)} collective-permute-done((bf16[1024,512]{1,0:T(8,128)(2,1)S(1)}, bf16[1024,512]{1,0:T(8,128)(2,1)S(1)}, u32[]{:S(2)}, u32[]{:S(2)}) %collective-permute-start) | collective-permute-done | bytes 1048608 | tf_op jit(solution)/shard_map/while/body/eval_jaxpr/ppermute | solution.py:10
  142.0 0.1 copy.37
  142.1 1.9 collective-permute-start
  144.0 15.1 %collective-permute-done = bf16[1024,512]{1,0:T(8,128)(2,1)S(1)} collective-permute-done((bf16[1024,512]{1,0:T(8,128)(2,1)S(1)}, bf16[1024,512]{1,0:T(8,128)(2,1)S(1)}, u32[]{:S(2)}, u32[]{:S(2)}) %collective-permute-start) | collective-permute-done | bytes 1048608 | tf_op jit(solution)/shard_map/while/body/eval_jaxpr/ppermute | solution.py:10
  159.1 0.1 copy.37
  159.2 1.9 collective-permute-start
  161.1 15.1 %collective-permute-done = bf16[1024,512]{1,0:T(8,128)(2,1)S(1)} collective-permute-done((bf16[1024,512]{1,0:T(8,128)(2,1)S(1)}, bf16[1024,512]{1,0:T(8,128)(2,1)S(1)}, u32[]{:S(2)}, u32[]{:S(2)}) %collective-permute-start) | collective-permute-done | bytes 1048608 | tf_op jit(solution)/shard_map/while/body/eval_jaxpr/ppermute | solution.py:10
  176.2 0.1 copy.37
  176.3 1.9 collective-permute-start
  178.3 30.8 %collective-permute-done = bf16[1024,512]{1,0:T(8,128)(2,1)S(1)} collective-permute-done((bf16[1024,512]{1,0:T(8,128)(2,1)S(1)}, bf16[1024,512]{1,0:T(8,128)(2,1)S(1)}, u32[]{:S(2)}, u32[]{:S(2)}) %collective-permute-start) | collective-permute-done | bytes 1048608 | tf_op jit(solution)/shard_map/while/body/eval_jaxpr/ppermute | solution.py:10
  209.0 0.1 copy.37
  209.1 15.3 %conditional.5 = ((bf16[1024,512]{1,0:T(8,128)(2,1)S(1)}, f32[3,1024,512]{2,1,0:T(8,128)})) conditional(s32[]{:T(128)} %convert_element_type.29, (bf16[1024,512]{1,0:T(8,128)(2,1)S(1)}, f32[3,1024,512]{2,1,0:T(8,128)}) %tuple.58, (s32[]{:T(128)}, bf16[1024,512]{1,0:T(8,128)(2,1)S(1)}, f32[3,1024,512]{2,1,0:T(8,128)}, ...), branch_computations={%region_1.1_spmd, %region_2.8_spmd} | conditional | flops 3222798336 | bytes 37748936 | solution.py:48
  209.8 4.4 %conditional = ((bf16[1024,512]{1,0:T(8,128)(2,1)S(1)}, f32[3,1024,512]{2,1,0:T(8,128)})) conditional(s32[]{:T(128)} %convert_element_type.23, (bf16[1024,512]{1,0:T(8,128)(2,1)S(1)}, f32[3,1024,512]{2,1,0:T(8,128)}) %tuple.36, (bf16[3,1024,1024]{2,1,0:T(8,128)(2,1)}, bf16[1024,512]{1,0:T(8,128)(2,1)S(1)}, f32[3,1024,512]{2,1,0:T(8,128)}) %tuple.37), branch_computations={%region_3.2_spmd, %region_4.3_spmd} | conditional | flops 1074266112 | bytes 12582936 | solution.py:23
  209.8 0.1 copy.39
  209.9 2.8 fusion.9
  212.7 1.5 bitcast_dynamic-update-slice_fusion
  214.9 4.4 %conditional.1 = ((bf16[1024,512]{1,0:T(8,128)(2,1)S(1)}, f32[3,1024,512]{2,1,0:T(8,128)})) conditional(s32[]{:T(128)} %convert_element_type.22, (bf16[1024,512]{1,0:T(8,128)(2,1)S(1)}, f32[3,1024,512]{2,1,0:T(8,128)}) %get-tuple-element.277, (bf16[3,1024,1024]{2,1,0:T(8,128)(2,1)}, bf16[1024,512]{1,0:T(8,128)(2,1)S(1)}, ...), branch_computations={%region_5.4_spmd, %region_6.5_spmd} | conditional | flops 1074266112 | bytes 12582936 | solution.py:23
  214.9 0.1 copy.40
  215.0 2.8 fusion.10
  217.8 1.5 bitcast_dynamic-update-slice_fusion.1
  220.0 4.4 %conditional.2 = ((bf16[1024,512]{1,0:T(8,128)(2,1)S(1)}, f32[3,1024,512]{2,1,0:T(8,128)})) conditional(s32[]{:T(128)} %convert_element_type.21, (bf16[1024,512]{1,0:T(8,128)(2,1)S(1)}, f32[3,1024,512]{2,1,0:T(8,128)}) %get-tuple-element.278, (bf16[3,1024,1024]{2,1,0:T(8,128)(2,1)}, bf16[1024,512]{1,0:T(8,128)(2,1)S(1)}, ...), branch_computations={%region_7.6_spmd, %region_8.7_spmd} | conditional | flops 1074266112 | bytes 12582936 | solution.py:23
  220.0 0.1 copy.41
  220.0 2.8 fusion.11
  222.9 1.5 bitcast_dynamic-update-slice_fusion.2
  224.4 1.9 collective-permute-start
  226.3 15.1 %collective-permute-done = bf16[1024,512]{1,0:T(8,128)(2,1)S(1)} collective-permute-done((bf16[1024,512]{1,0:T(8,128)(2,1)S(1)}, bf16[1024,512]{1,0:T(8,128)(2,1)S(1)}, u32[]{:S(2)}, u32[]{:S(2)}) %collective-permute-start) | collective-permute-done | bytes 1048608 | tf_op jit(solution)/shard_map/while/body/eval_jaxpr/ppermute | solution.py:10
  241.5 1.9 collective-permute-start
  243.4 15.1 %collective-permute-done = bf16[1024,512]{1,0:T(8,128)(2,1)S(1)} collective-permute-done((bf16[1024,512]{1,0:T(8,128)(2,1)S(1)}, bf16[1024,512]{1,0:T(8,128)(2,1)S(1)}, u32[]{:S(2)}, u32[]{:S(2)}) %collective-permute-start) | collective-permute-done | bytes 1048608 | tf_op jit(solution)/shard_map/while/body/eval_jaxpr/ppermute | solution.py:10
  258.6 1.9 collective-permute-start
  260.6 15.1 %collective-permute-done = bf16[1024,512]{1,0:T(8,128)(2,1)S(1)} collective-permute-done((bf16[1024,512]{1,0:T(8,128)(2,1)S(1)}, bf16[1024,512]{1,0:T(8,128)(2,1)S(1)}, u32[]{:S(2)}, u32[]{:S(2)}) %collective-permute-start) | collective-permute-done | bytes 1048608 | tf_op jit(solution)/shard_map/while/body/eval_jaxpr/ppermute | solution.py:10
  275.8 1.9 collective-permute-start
  277.7 15.1 %collective-permute-done = bf16[1024,512]{1,0:T(8,128)(2,1)S(1)} collective-permute-done((bf16[1024,512]{1,0:T(8,128)(2,1)S(1)}, bf16[1024,512]{1,0:T(8,128)(2,1)S(1)}, u32[]{:S(2)}, u32[]{:S(2)}) %collective-permute-start) | collective-permute-done | bytes 1048608 | tf_op jit(solution)/shard_map/while/body/eval_jaxpr/ppermute | solution.py:10
  (17 shorter events, 0.4 us)
Async XLA Ops:
  0.0 113.0 %copy-start.1 = (bf16[3,256,1024]{2,1,0:T(8,128)(2,1)S(1)}, bf16[3,256,1024]{2,1,0:T(8,128)(2,1)}, u32[]{:S(2)}) copy-start(bf16[3,256,1024]{2,1,0:T(8,128)(2,1)} %param.13) | copy-start | bytes 4718596
  0.0 37.6 %collective-permute-start.1 = (bf16[3,256,1024]{2,1,0:T(8,128)(2,1)}, bf16[3,256,1024]{2,1,0:T(8,128)(2,1)S(1)}, u32[]{:S(2)}, u32[]{:S(2)}) collective-permute-start(bf16[3,256,1024]{2,1,0:T(8,128)(2,1)} %param.13), channel_id=1, source_target_pairs={{0,1},{1,2},{2,3},{3,0},{4,5},{5,6},{6,7},{7,4},{8,9},{9,10},{10,1... | collective-permute-start | bytes 4718600 | tf_op jit(solution)/shard_map/ppermute | solution.py:39
  37.6 36.5 %collective-permute-start.2 = (bf16[3,256,1024]{2,1,0:T(8,128)(2,1)S(1)}, bf16[3,256,1024]{2,1,0:T(8,128)(2,1)}, u32[]{:S(2)}, u32[]{:S(2)}) collective-permute-start(bf16[3,256,1024]{2,1,0:T(8,128)(2,1)S(1)} %collective-permute-done.1), channel_id=1, source_target_pairs={{0,1},{1,2},{2,3},{3,0},{4,5},{5,6},{6,7},{7,4},{8,9},{9,10},{10,1... | collective-permute-start | bytes 4718600 | tf_op jit(solution)/shard_map/ppermute | solution.py:39
  74.0 35.8 %collective-permute-start.3 = (bf16[3,256,1024]{2,1,0:T(8,128)(2,1)}, bf16[3,256,1024]{2,1,0:T(8,128)(2,1)}, u32[]{:S(2)}, u32[]{:S(2)}) collective-permute-start(bf16[3,256,1024]{2,1,0:T(8,128)(2,1)} %collective-permute-done.2), channel_id=1, source_target_pairs={{0,1},{1,2},{2,3},{3,0},{4,5},{5,6},{6,7},{7,4},{8,9},{9,10},{10,1... | collective-permute-start | bytes 4718600 | tf_op jit(solution)/shard_map/ppermute | solution.py:39
  119.9 3.5 %copy-start = (bf16[1024,512]{1,0:T(8,128)(2,1)S(1)}, bf16[1024,512]{1,0:T(8,128)(2,1)}, u32[]{:S(2)}) copy-start(bf16[1024,512]{1,0:T(8,128)(2,1)} %param.15) | copy-start | bytes 3145732
  123.4 18.6 %collective-permute-start = (bf16[1024,512]{1,0:T(8,128)(2,1)S(1)}, bf16[1024,512]{1,0:T(8,128)(2,1)S(1)}, u32[]{:S(2)}, u32[]{:S(2)}) collective-permute-start(bf16[1024,512]{1,0:T(8,128)(2,1)S(1)} %get-tuple-element.235), channel_id=1, source_target_pairs={{4,0},{8,4},{12,8},{16,12},{20,16},{24,20},{28,24},{5,1},{9,5},{13... | collective-permute-start | bytes 3145736 | tf_op jit(solution)/shard_map/while/body/eval_jaxpr/ppermute | solution.py:10
  142.1 17.0 %collective-permute-start = (bf16[1024,512]{1,0:T(8,128)(2,1)S(1)}, bf16[1024,512]{1,0:T(8,128)(2,1)S(1)}, u32[]{:S(2)}, u32[]{:S(2)}) collective-permute-start(bf16[1024,512]{1,0:T(8,128)(2,1)S(1)} %get-tuple-element.235), channel_id=1, source_target_pairs={{4,0},{8,4},{12,8},{16,12},{20,16},{24,20},{28,24},{5,1},{9,5},{13... | collective-permute-start | bytes 3145736 | tf_op jit(solution)/shard_map/while/body/eval_jaxpr/ppermute | solution.py:10
  159.2 17.0 %collective-permute-start = (bf16[1024,512]{1,0:T(8,128)(2,1)S(1)}, bf16[1024,512]{1,0:T(8,128)(2,1)S(1)}, u32[]{:S(2)}, u32[]{:S(2)}) collective-permute-start(bf16[1024,512]{1,0:T(8,128)(2,1)S(1)} %get-tuple-element.235), channel_id=1, source_target_pairs={{4,0},{8,4},{12,8},{16,12},{20,16},{24,20},{28,24},{5,1},{9,5},{13... | collective-permute-start | bytes 3145736 | tf_op jit(solution)/shard_map/while/body/eval_jaxpr/ppermute | solution.py:10
  176.3 32.7 %collective-permute-start = (bf16[1024,512]{1,0:T(8,128)(2,1)S(1)}, bf16[1024,512]{1,0:T(8,128)(2,1)S(1)}, u32[]{:S(2)}, u32[]{:S(2)}) collective-permute-start(bf16[1024,512]{1,0:T(8,128)(2,1)S(1)} %get-tuple-element.235), channel_id=1, source_target_pairs={{4,0},{8,4},{12,8},{16,12},{20,16},{24,20},{28,24},{5,1},{9,5},{13... | collective-permute-start | bytes 3145736 | tf_op jit(solution)/shard_map/while/body/eval_jaxpr/ppermute | solution.py:10
  224.4 17.0 %collective-permute-start = (bf16[1024,512]{1,0:T(8,128)(2,1)S(1)}, bf16[1024,512]{1,0:T(8,128)(2,1)S(1)}, u32[]{:S(2)}, u32[]{:S(2)}) collective-permute-start(bf16[1024,512]{1,0:T(8,128)(2,1)S(1)} %get-tuple-element.235), channel_id=1, source_target_pairs={{4,0},{8,4},{12,8},{16,12},{20,16},{24,20},{28,24},{5,1},{9,5},{13... | collective-permute-start | bytes 3145736 | tf_op jit(solution)/shard_map/while/body/eval_jaxpr/ppermute | solution.py:10
  241.5 17.0 %collective-permute-start = (bf16[1024,512]{1,0:T(8,128)(2,1)S(1)}, bf16[1024,512]{1,0:T(8,128)(2,1)S(1)}, u32[]{:S(2)}, u32[]{:S(2)}) collective-permute-start(bf16[1024,512]{1,0:T(8,128)(2,1)S(1)} %get-tuple-element.235), channel_id=1, source_target_pairs={{4,0},{8,4},{12,8},{16,12},{20,16},{24,20},{28,24},{5,1},{9,5},{13... | collective-permute-start | bytes 3145736 | tf_op jit(solution)/shard_map/while/body/eval_jaxpr/ppermute | solution.py:10
  258.6 17.0 %collective-permute-start = (bf16[1024,512]{1,0:T(8,128)(2,1)S(1)}, bf16[1024,512]{1,0:T(8,128)(2,1)S(1)}, u32[]{:S(2)}, u32[]{:S(2)}) collective-permute-start(bf16[1024,512]{1,0:T(8,128)(2,1)S(1)} %get-tuple-element.235), channel_id=1, source_target_pairs={{4,0},{8,4},{12,8},{16,12},{20,16},{24,20},{28,24},{5,1},{9,5},{13... | collective-permute-start | bytes 3145736 | tf_op jit(solution)/shard_map/while/body/eval_jaxpr/ppermute | solution.py:10
  275.8 17.0 %collective-permute-start = (bf16[1024,512]{1,0:T(8,128)(2,1)S(1)}, bf16[1024,512]{1,0:T(8,128)(2,1)S(1)}, u32[]{:S(2)}, u32[]{:S(2)}) collective-permute-start(bf16[1024,512]{1,0:T(8,128)(2,1)S(1)} %get-tuple-element.235), channel_id=1, source_target_pairs={{4,0},{8,4},{12,8},{16,12},{20,16},{24,20},{28,24},{5,1},{9,5},{13... | collective-permute-start | bytes 3145736 | tf_op jit(solution)/shard_map/while/body/eval_jaxpr/ppermute | solution.py:10
